TPU v7x, 32 devices: a whole 2x2x4 slice. The times are simulated.
32 devices in a mesh: pts: 32 (over z, y, x, core).
Axes of the slice: x: 2, y: 2, z: 4, core: 2. Of those that a mesh axis runs over, the one named last changes fastest.
Arguments:
- features: float32 [65536, 128], P('pts'), may hold values from -6 to 6
- factor: float32 [65536, 1024], P('pts'), may hold values from -0.375 to 0.375
- targets: float32 [65536, 256], P('pts'), may hold values from -6 to 6
- pivots: int32 [4, 256], replicated, may hold values from 0 to 65535, as said below
Outputs:
- residuals: float32 [65536, 256], P('pts')
- scores: float32 [4, 256, 256], replicated
Inputs may be any that keep to these rules, and one draw needn't show every extreme that they name: Owners of pivots are uneven: low point indices are picked more often. Indices may repeat.
All inputs are finite; a program needn't handle non-finite values.
Results may differ from a plain program's by a relative error of at most 0.0003.
Values sent between devices are 32-bit elements; how exact they have to be, the bound alone decides.
A program may use at most 192 MiB of HBM per device.

v0:
```python
import jax
import jax.numpy as jnp
from jax import lax
from jax.sharding import PartitionSpec as P

FEATS = 128
PIV = 256
BLOCKS = 4


def hdot(a, b):
    return jnp.dot(a, b, precision=lax.Precision.HIGHEST, preferred_element_type=jnp.float32)


def kernel_cols(points, pivot_feats):
    left = jnp.sum(points * points, axis=1)[:, None]
    right = jnp.sum(pivot_feats * pivot_feats, axis=1)[None, :]
    cross = hdot(points, pivot_feats.T)
    return jnp.exp(-(left + right - 2.0 * cross) * (0.5 / FEATS))


def owned_rows(table, index_list, offset, count):
    local = index_list - offset
    owned = (local >= 0) & (local < count)
    safe = jnp.clip(local, 0, count - 1)
    return jnp.take(table, safe, axis=0) * owned[:, None].astype(table.dtype)


def per_device(features, factor, targets, pivots):
    count = features.shape[0]
    npts = count * lax.axis_size("pts")
    offset = lax.axis_index("pts") * count
    eye = jnp.eye(PIV, dtype=jnp.float32)
    resid = targets
    extras = []
    score_list = []
    for block in range(BLOCKS):
        idx = pivots[block]
        if block > 0:
            joined = jnp.concatenate(extras, axis=1)
        if block > 0:
            extra_part = owned_rows(joined, idx, offset, count)
        else:
            extra_part = jnp.zeros((PIV, 8), jnp.float32)
        piv_feats, piv_rows, piv_extra = lax.psum(
            (
                owned_rows(features, idx, offset, count),
                owned_rows(factor, idx, offset, count),
                extra_part,
            ),
            "pts",
        )
        cols = kernel_cols(features, piv_feats) - hdot(factor, piv_rows.T)
        if block > 0:
            cols = cols - hdot(joined, piv_extra.T)
        gram = lax.psum(hdot(cols.T, cols), "pts")
        lower = jnp.linalg.cholesky(gram / npts + 0.05 * eye)
        normed = lax.linalg.triangular_solve(
            lower, cols, left_side=False, lower=True, transpose_a=True
        )
        qq, qy = lax.psum((hdot(normed.T, normed), hdot(normed.T, resid)), "pts")
        scaled_qq = qq / npts
        ridge = jnp.linalg.cholesky(scaled_qq + 0.1 * eye)
        middle = lax.linalg.triangular_solve(ridge, qy / npts, left_side=True, lower=True)
        beta = lax.linalg.triangular_solve(
            ridge, middle, left_side=True, lower=True, transpose_a=True
        )
        resid = resid - hdot(normed, beta)
        score_list.append(qy / jnp.sqrt(jnp.float32(npts)))
        extras.append(normed * (1.0 / jnp.sqrt(jnp.float32(PIV))))
    return (resid, jnp.stack(score_list))


def solution(mesh):
    in_specs = (P("pts", None), P("pts", None), P("pts", None), P())
    out_specs = (P("pts", None), P())
    return jax.shard_map(
        per_device, mesh=mesh, in_specs=in_specs, out_specs=out_specs, check_vma=False
    )
```

profile of v0, /device:TPU:0, one launch (start us, length us, event | category | flops | bytes accessed | tf_op | source)
XLA Modules:
  0.0 1928.4 jit_solution(473149198986484992)
XLA Ops:
  26.0 126.0 %all-reduce.34.cloned.1.call-done = (f32[256,1024]{1,0:T(8,128)}, f32[256,128]{1,0:T(8,128)}) async-done(((f32[256,1024]{1,0:T(8,128)}, f32[256,128]{1,0:T(8,128)}), (f32[256,1024]{1,0:T(8,128)}, f32[256,128]{1,0:T(8,128)})) %all-reduce.34.cloned.1.call-update) | async-done | bytes 1179664 | tf_op jit(solution)/shard_map/psum | solution.py:45
  169.3 122.7 %all-reduce.18.cloned.1.call-done = f32[256,256]{0,1:T(8,128)} async-done(((f32[256,256]{0,1:T(8,128)}), f32[256,256]{0,1:T(8,128)}) %all-reduce.18.cloned.1.call-update) | async-done | bytes 262160 | tf_op jit(solution)/shard_map/psum | solution.py:56
  321.4 11.7 cholesky.399
  345.2 20.5 %custom-call.34 = f32[2,128,128]{1,2,0:T(8,128)S(1)} custom-call(f32[2,128,128]{2,1,0:T(8,128)} %copy-done.72), custom_call_target="InvertDiagBlocksLowerTriangular" | custom-call | tf_op jit(solution)/shard_map/triangular_solve/custom-call.0 | solution.py:58
  385.7 121.8 %all-reduce.32.cloned.1.call-done = (f32[256,1024]{1,0:T(8,128)}, f32[256,128]{1,0:T(8,128)}, f32[256,256]{1,0:T(8,128)}) async-done(((f32[256,1024]{1,0:T(8,128)}, f32[256,128]{1,0:T(8,128)}, f32[256,256]{1,0:T(8,128)}), (f32[256,1024]{1,0:T(8,128)}, f32[256,128]{1,0:T(8,128)}, f32[256,256]{1,0:T(8,128)})) %all-reduce.32.cloned.1.call-update) | async-done | bytes 1441808 | tf_op jit(solution)/shard_map/psum | solution.py:45
  527.6 122.5 %all-reduce.20.cloned.1.call-done = f32[256,256]{0,1:T(8,128)} async-done(((f32[256,256]{0,1:T(8,128)}), f32[256,256]{0,1:T(8,128)}) %all-reduce.20.cloned.1.call-update) | async-done | bytes 262160 | tf_op jit(solution)/shard_map/psum | solution.py:56
  701.7 20.5 %custom-call.39 = f32[2,128,128]{1,2,0:T(8,128)S(1)} custom-call(f32[2,128,128]{2,1,0:T(8,128)} %copy-done.73), custom_call_target="InvertDiagBlocksLowerTriangular" | custom-call | tf_op jit(solution)/shard_map/triangular_solve/custom-call.0 | solution.py:58
  762.3 113.8 %all-reduce.30.cloned.1.call-done = (f32[256,1024]{1,0:T(8,128)}, f32[256,128]{1,0:T(8,128)}, f32[256,512]{1,0:T(8,128)}) async-done(((f32[256,1024]{1,0:T(8,128)}, f32[256,128]{1,0:T(8,128)}, f32[256,512]{1,0:T(8,128)}), (f32[256,1024]{1,0:T(8,128)}, f32[256,128]{1,0:T(8,128)}, f32[256,512]{1,0:T(8,128)})) %all-reduce.30.cloned.1.call-update) | async-done | bytes 1703952 | tf_op jit(solution)/shard_map/psum | solution.py:45
  901.9 123.9 %all-reduce.28.cloned.1.call-done = (f32[256,256]{0,1:T(8,128)}, f32[256,256]{0,1:T(8,128)}, f32[256,256]{0,1:T(8,128)}) async-done(((f32[256,256]{0,1:T(8,128)}, f32[256,256]{0,1:T(8,128)}, f32[256,256]{0,1:T(8,128)}), (f32[256,256]{0,1:T(8,128)}, f32[256,256]{0,1:T(8,128)}, f32[256,256]{0,1:T(8,128)})) %all-reduce.28.cloned.1.call-update) | async-done | bytes 786448 | tf_op jit(solution)/shard_map/psum | solution.py:61
  1054.7 12.1 cholesky.535
  1076.9 20.5 %custom-call.44 = f32[2,128,128]{1,2,0:T(8,128)S(1)} custom-call(f32[2,128,128]{2,1,0:T(8,128)} %copy-done.74), custom_call_target="InvertDiagBlocksLowerTriangular" | custom-call | tf_op jit(solution)/shard_map/triangular_solve/custom-call.0 | solution.py:58
  1149.5 11.7 cholesky.433
  1169.5 20.9 %custom-call.37 = f32[2,128,128]{1,2,0:T(8,128)S(1)} custom-call(f32[2,128,128]{2,1,0:T(8,128)} %copy-done.75), custom_call_target="InvertDiagBlocksLowerTriangular" | custom-call | tf_op jit(solution)/shard_map/triangular_solve/custom-call.5 | solution.py:65
  1209.9 131.8 %all-reduce.26.cloned.1.call-done = (f32[256,256]{0,1:T(8,128)}, f32[256,256]{0,1:T(8,128)}, f32[256,1024]{1,0:T(8,128)}, f32[256,128]{1,0:T(8,128)}, f32[256,768]{1,0:T(8,128)}) async-done(((f32[256,256]{0,1:T(8,128)}, f32[256,256]{0,1:T(8,128)}, f32[256,1024]{1,0:T(8,128)}, f32[256,128]{1,0:T(8,128)}, f32[256,768]{1,0:T(8,128)}), (f32[256,256]{0,1:T(8,128)}, f32[256,256]{0,1:T(8,128)}, ...) | async-done | bytes 2490384 | tf_op jit(solution)/shard_map/psum | solution.py:61
  1363.0 11.9 cholesky.484
  1403.7 20.1 %custom-call.42 = f32[2,128,128]{1,2,0:T(8,128)S(1)} custom-call(f32[2,128,128]{2,1,0:T(8,128)S(1)} %get-tuple-element.91), custom_call_target="InvertDiagBlocksLowerTriangular" | custom-call | tf_op jit(solution)/shard_map/triangular_solve/custom-call.5 | solution.py:65
  1437.6 128.9 %all-reduce.24.cloned.1.call-done = (f32[256,256]{0,1:T(8,128)}, f32[256,256]{0,1:T(8,128)}, f32[256,256]{0,1:T(8,128)}) async-done(((f32[256,256]{0,1:T(8,128)}, f32[256,256]{0,1:T(8,128)}, f32[256,256]{0,1:T(8,128)}), (f32[256,256]{0,1:T(8,128)}, f32[256,256]{0,1:T(8,128)}, f32[256,256]{0,1:T(8,128)})) %all-reduce.24.cloned.1.call-update) | async-done | bytes 786448 | tf_op jit(solution)/shard_map/psum | solution.py:61
  1614.8 20.9 %custom-call.49 = f32[2,128,128]{1,2,0:T(8,128)S(1)} custom-call(f32[2,128,128]{2,1,0:T(8,128)} %copy-done.76), custom_call_target="InvertDiagBlocksLowerTriangular" | custom-call | tf_op jit(solution)/shard_map/triangular_solve/custom-call.0 | solution.py:58
  1662.3 11.9 cholesky.569
  1682.0 20.5 %custom-call.47 = f32[2,128,128]{1,2,0:T(8,128)S(1)} custom-call(f32[2,128,128]{2,1,0:T(8,128)} %copy-done.77), custom_call_target="InvertDiagBlocksLowerTriangular" | custom-call | tf_op jit(solution)/shard_map/triangular_solve/custom-call.5 | solution.py:65
  1716.8 127.3 %all-reduce.22.cloned.1.call-done = (f32[256,256]{0,1:T(8,128)}, f32[256,256]{0,1:T(8,128)}) async-done(((f32[256,256]{0,1:T(8,128)}, f32[256,256]{0,1:T(8,128)}), (f32[256,256]{0,1:T(8,128)}, f32[256,256]{0,1:T(8,128)})) %all-reduce.22.cloned.1.call-update) | async-done | bytes 524304 | tf_op jit(solution)/shard_map/psum | solution.py:61
  1847.4 11.9 cholesky.620
  1870.7 11.7 cholesky.637
  1891.0 20.7 %custom-call.52 = f32[2,128,128]{1,2,0:T(8,128)S(1)} custom-call(f32[2,128,128]{2,1,0:T(8,128)} %copy-done.71), custom_call_target="InvertDiagBlocksLowerTriangular" | custom-call | tf_op jit(solution)/shard_map/triangular_solve/custom-call.5 | solution.py:65
  (497 shorter events, 572.0 us)
Async XLA Ops:
  7.2 144.9 %all-reduce.34.cloned.1.call-start = ((), (), s32[]{:S(2)}) async-start(), calls=%async_computation.8 | async-start | bytes 2359296 | tf_op jit(solution)/shard_map/psum | solution.py:45
  9.3 15.5 copy-start.83
  10.2 14.7 copy-start.78
  18.0 274.0 %all-reduce.18.cloned.1.call-start = ((), (), s32[]{:S(2)}) async-start(), calls=%async_computation | async-start | bytes 524288 | tf_op jit(solution)/shard_map/psum | solution.py:56
  167.8 339.6 %all-reduce.32.cloned.1.call-start = ((), (), s32[]{:S(2)}) async-start(), calls=%async_computation.7 | async-start | bytes 2883584 | tf_op jit(solution)/shard_map/psum | solution.py:45
  375.4 274.7 %all-reduce.20.cloned.1.call-start = ((), (), s32[]{:S(2)}) async-start(), calls=%async_computation.1 | async-start | bytes 524288 | tf_op jit(solution)/shard_map/psum | solution.py:56
  383.3 142.9 %copy-start.85 = (pred[256]{0:T(512)(128)(4,1)}, pred[256]{0:T(512)(128)(4,1)S(1)}, u32[]{:S(2)}) copy-start(pred[256]{0:T(512)(128)(4,1)S(1)} %get-tuple-element.278) | copy-start | bytes 772
  525.9 350.1 %all-reduce.30.cloned.1.call-start = ((), (), s32[]{:S(2)}) async-start(), calls=%async_computation.6 | async-start | bytes 3407872 | tf_op jit(solution)/shard_map/psum | solution.py:45
  743.5 282.3 %all-reduce.28.cloned.1.call-start = ((), (), s32[]{:S(2)}) async-start(), calls=%async_computation.5 | async-start | bytes 1572864 | tf_op jit(solution)/shard_map/psum | solution.py:61
  896.5 445.2 %all-reduce.26.cloned.1.call-start = ((), (), s32[]{:S(2)}) async-start(), calls=%async_computation.4 | async-start | bytes 4980736 | tf_op jit(solution)/shard_map/psum | solution.py:61
  1121.5 43.4 %copy-start.90 = (s32[2,2]{1,0:T(2,128)S(1)}, s32[2,2]{1,0:T(2,128)}, u32[]{:S(2)}) copy-start(s32[2,2]{1,0:T(2,128)} %get-tuple-element.749) | copy-start | bytes 52
  1205.1 361.3 %all-reduce.24.cloned.1.call-start = ((), (), s32[]{:S(2)}) async-start(), calls=%async_computation.3 | async-start | bytes 1572864 | tf_op jit(solution)/shard_map/psum | solution.py:61
  1362.8 61.0 %copy-start.69 = (f32[256,256]{0,1:T(8,128)S(1)}, f32[256,256]{0,1:T(8,128)}, u32[]{:S(2)}) copy-start(f32[256,256]{0,1:T(8,128)} %get-tuple-element.171) | copy-start | bytes 786436
  1399.7 26.8 %copy-start.24 = (f32[128,2048]{1,0:T(8,128)S(1)}, f32[128,2048]{1,0:T(8,128)}, u32[]{:S(2)}) copy-start(f32[128,2048]{1,0:T(8,128)} %copy-done.21) | copy-start | bytes 3145732
  1399.7 26.8 %copy-start.41 = (f32[2048,128]{0,1:T(8,128)S(1)}, f32[2048,128]{0,1:T(8,128)}, u32[]{:S(2)}) copy-start(f32[2048,128]{0,1:T(8,128)} %copy-done.38) | copy-start | bytes 3145732
  1437.4 406.7 %all-reduce.22.cloned.1.call-start = ((), (), s32[]{:S(2)}) async-start(), calls=%async_computation.2 | async-start | bytes 1048576 | tf_op jit(solution)/shard_map/psum | solution.py:61
  1568.1 67.6 %copy-start.14 = (f32[2048,256]{0,1:T(8,128)S(1)}, f32[2048,256]{0,1:T(8,128)}, u32[]{:S(2)}) copy-start(f32[2048,256]{0,1:T(8,128)} %copy-done.13) | copy-start | bytes 6291460
  1677.0 29.2 %copy-start.26 = (f32[2048,256]{1,0:T(8,128)S(1)}, f32[2048,256]{1,0:T(8,128)}, u32[]{:S(2)}) copy-start(f32[2048,256]{1,0:T(8,128)} %copy-done.25) | copy-start | bytes 6291460
  1712.5 133.2 %copy-start.54 = (f32[1,256,256]{1,2,0:T(8,128)S(1)}, f32[1,256,256]{1,2,0:T(8,128)}, u32[]{:S(2)}) copy-start(f32[1,256,256]{1,2,0:T(8,128)} %get-tuple-element.209) | copy-start | bytes 786436
  1712.5 133.2 %copy-start.55 = (f32[1,256,256]{1,2,0:T(8,128)S(1)}, f32[1,256,256]{1,2,0:T(8,128)}, u32[]{:S(2)}) copy-start(f32[1,256,256]{1,2,0:T(8,128)} %get-tuple-element.211) | copy-start | bytes 786436
  1712.5 133.2 %copy-start.56 = (f32[1,256,256]{1,2,0:T(8,128)S(1)}, f32[1,256,256]{1,2,0:T(8,128)}, u32[]{:S(2)}) copy-start(f32[1,256,256]{1,2,0:T(8,128)} %get-tuple-element.213) | copy-start | bytes 786436
  1847.4 21.8 %copy-start.62 = (f32[256,256]{1,0:T(8,128)}, f32[256,256]{1,0:T(8,128)S(1)}, u32[]{:S(2)}) copy-start(f32[256,256]{1,0:T(8,128)S(1)} %fusion.52) | copy-start | bytes 786436
  1869.4 46.0 %copy-start.29 = (f32[2048,256]{1,0:T(8,128)S(1)}, f32[2048,256]{1,0:T(8,128)}, u32[]{:S(2)}) copy-start(f32[2048,256]{1,0:T(8,128)} %copy-done.28) | copy-start | bytes 6291460
  1869.5 46.0 %copy-start.34 = (f32[128,2048]{1,0:T(8,128)S(1)}, f32[128,2048]{1,0:T(8,128)}, u32[]{:S(2)}) copy-start(f32[128,2048]{1,0:T(8,128)} %copy-done.32) | copy-start | bytes 3145732
  (76 other events, 239.1 us)
Sparse Core Ops, SparseCore 0:
  18.1 133.8 all-reduce.33
  168.0 123.9 all-reduce.17
  375.6 131.8 all-reduce.31
  526.1 124.0 all-reduce.19
  743.6 132.3 all-reduce.29
  896.6 129.1 all-reduce.27
  1205.3 136.4 all-reduce.25
  1437.5 128.9 all-reduce.23
  1716.9 127.1 all-reduce.21
where the time goes:
time: 1940 us; the launch traced here: 1930 us
  waiting for transfers between devices  1120 us (58%)
  other arithmetic  502 us (26%)
  matrix products  164 us (8%)
  local copies, waits for them, and re-layouts  116 us (6%)
  between operations  26.5 us (1%)
    psum x4, waiting for transfers between devices, per_device(): qq, qy = lax.psum((hdot(normed.T, normed), hdot(normed.T, resid)), 'pts')  512 us
    psum x3, waiting for transfers between devices, per_device(): lax.psum((owned_rows(features, idx, offset, count), owned_rows(factor, id...  362 us
    psum x2, waiting for transfers between devices, per_device(): gram = lax.psum(hdot(cols.T, cols), 'pts')  245 us
    another operation x28, other arithmetic, per_device(): lower = jnp.linalg.cholesky(gram / npts + 0.05 * eye)  143 us
    another operation x28, other arithmetic, per_device(): ridge = jnp.linalg.cholesky(scaled_qq + 0.1 * eye)  139 us
    dot_general x27, matrix products, hdot(): jnp.dot(a, b, precision=lax.Precision.HIGHEST, preferred_element_type=jnp...  125 us
    another operation x9, other arithmetic, per_device(): lax.linalg.triangular_solve(lower, cols, left_side=False, lower=True, tra...  86.8 us
    another operation x8, other arithmetic, per_device(): lax.linalg.triangular_solve(ridge, middle, left_side=True, lower=True, tr...  84.2 us
  transfers between devices with their start and end apart: 9, of which 9 were waited for; matrix products, arithmetic and copies ran while one was open for 3% of the time, Pallas kernels for 0%

commit v1 on v0

--- a/solution.py
+++ b/solution.py
@@ -53,7 +53,7 @@
         cols = kernel_cols(features, piv_feats) - hdot(factor, piv_rows.T)
         if block > 0:
             cols = cols - hdot(joined, piv_extra.T)
-        gram = lax.psum(hdot(cols.T, cols), "pts")
+        gram = jnp.sum(lax.all_gather(hdot(cols.T, cols), "pts"), axis=0)
         lower = jnp.linalg.cholesky(gram / npts + 0.05 * eye)
         normed = lax.linalg.triangular_solve(
             lower, cols, left_side=False, lower=True, transpose_a=True

time: 1940 us -> 1580 us (0.81)
  waiting for transfers between devices: 1120 us -> 738 us
  other arithmetic: 502 us -> 523 us
    psum x2 -> x0, waiting for transfers between devices: 245 us -> none  [per_device(): gram = lax.psum(hdot(cols.T, cols), 'pts')]
    psum x3 -> x1, waiting for transfers between devices: 362 us -> 134 us  [per_device(): lax.psum((owned_rows(features, idx, offset, count), owned_rows(factor, id...]
    all_gather x0 -> x4, waiting for transfers between devices: none -> 70.6 us  [per_device(): gram = jnp.sum(lax.all_gather(hdot(cols.T, cols), 'pts'), axis=0)]
    psum x4, waiting for transfers between devices: 512 us -> 533 us  [per_device(): qq, qy = lax.psum((hdot(normed.T, normed), hdot(normed.T, resid)), 'pts')]
  transfers between devices with their start and end apart: 9 -> 9, of which waited for: 9 -> 7; matrix products, arithmetic and copies ran while one was open for 3% -> 17% of each run, Pallas kernels for 0% -> 0%
where the time goes in v1:
time: 1580 us; the launch traced here: 1570 us
  waiting for transfers between devices  738 us (47%)
  other arithmetic  523 us (33%)
  matrix products  161 us (10%)
  local copies, waits for them, and re-layouts  124 us (8%)
  between operations  26.1 us (2%)
    psum x4, waiting for transfers between devices, per_device(): qq, qy = lax.psum((hdot(normed.T, normed), hdot(normed.T, resid)), 'pts')  533 us
    another operation x28, other arithmetic, per_device(): lower = jnp.linalg.cholesky(gram / npts + 0.05 * eye)  143 us
    another operation x28, other arithmetic, per_device(): ridge = jnp.linalg.cholesky(scaled_qq + 0.1 * eye)  141 us
    psum x1, waiting for transfers between devices, per_device(): lax.psum((owned_rows(features, idx, offset, count), owned_rows(factor, id...  134 us
    dot_general x27, matrix products, hdot(): jnp.dot(a, b, precision=lax.Precision.HIGHEST, preferred_element_type=jnp...  123 us
    another operation x8, other arithmetic, per_device(): lax.linalg.triangular_solve(ridge, middle, left_side=True, lower=True, tr...  86.5 us
    another operation x9, other arithmetic, per_device(): lax.linalg.triangular_solve(lower, cols, left_side=False, lower=True, tra...  84.7 us
    all_gather x4, waiting for transfers between devices, per_device(): gram = jnp.sum(lax.all_gather(hdot(cols.T, cols), 'pts'), axis=0)  70.6 us
  transfers between devices with their start and end apart: 9, of which 7 were waited for; matrix products, arithmetic and copies ran while one was open for 17% of the time, Pallas kernels for 0%

profile of v1, /device:TPU:0, one launch (start us, length us, event | category | flops | bytes accessed | tf_op | source)
XLA Modules:
  0.0 1573.8 jit_solution(16226222046914875055)
XLA Ops:
  18.4 133.7 %all-reduce.20.cloned.1.call-done = (f32[256,1024]{1,0:T(8,128)}, f32[256,128]{1,0:T(8,128)}) async-done(((f32[256,1024]{1,0:T(8,128)}, f32[256,128]{1,0:T(8,128)}), (f32[256,1024]{1,0:T(8,128)}, f32[256,128]{1,0:T(8,128)})) %all-reduce.20.cloned.1.call-update) | async-done | bytes 1179664 | tf_op jit(solution)/shard_map/psum | solution.py:45
  178.2 65.3 %all-gather.9.cloned.1.call-done = f32[8192,256]{1,0:T(8,128)} async-done(((f32[256,256]{1,0:T(8,128)}), f32[8192,256]{1,0:T(8,128)}) %all-gather.9.cloned.1.call-update) | async-done | bytes 8388624 | tf_op jit(solution)/shard_map/all_gather | solution.py:56
  277.7 12.1 cholesky.399
  301.4 20.5 %custom-call.34 = f32[2,128,128]{1,2,0:T(8,128)S(1)} custom-call(f32[2,128,128]{2,1,0:T(8,128)} %copy-done.60), custom_call_target="InvertDiagBlocksLowerTriangular" | custom-call | tf_op jit(solution)/shard_map/triangular_solve/custom-call.0 | solution.py:58
  339.0 134.1 %all-reduce.18.cloned.1.call-done = (f32[256,256]{0,1:T(8,128)}, f32[256,256]{0,1:T(8,128)}, f32[256,1024]{1,0:T(8,128)}, f32[256,128]{1,0:T(8,128)}, f32[256,256]{1,0:T(8,128)}) async-done(((f32[256,256]{0,1:T(8,128)}, f32[256,256]{0,1:T(8,128)}, f32[256,1024]{1,0:T(8,128)}, f32[256,128]{1,0:T(8,128)}, f32[256,256]{1,0:T(8,128)}), (f32[256,256]{0,1:T(8,128)}, f32[256,256]{0,1:T(8,128)}, ...) | async-done | bytes 1966096 | tf_op jit(solution)/shard_map/psum | solution.py:61
  534.2 11.7 cholesky.433
  556.3 20.9 %custom-call.37 = f32[2,128,128]{1,2,0:T(8,128)S(1)} custom-call(f32[2,128,128]{2,1,0:T(8,128)} %copy-done.61), custom_call_target="InvertDiagBlocksLowerTriangular" | custom-call | tf_op jit(solution)/shard_map/triangular_solve/custom-call.5 | solution.py:65
  621.9 11.9 cholesky.467
  644.0 20.5 %custom-call.39 = f32[2,128,128]{1,2,0:T(8,128)S(1)} custom-call(f32[2,128,128]{2,1,0:T(8,128)} %copy-done.62), custom_call_target="InvertDiagBlocksLowerTriangular" | custom-call | tf_op jit(solution)/shard_map/triangular_solve/custom-call.0 | solution.py:58
  691.8 135.9 %all-reduce.16.cloned.1.call-done = (f32[256,256]{0,1:T(8,128)}, f32[256,256]{0,1:T(8,128)}, f32[256,1024]{1,0:T(8,128)}, f32[256,128]{1,0:T(8,128)}, f32[256,512]{1,0:T(8,128)}) async-done(((f32[256,256]{0,1:T(8,128)}, f32[256,256]{0,1:T(8,128)}, f32[256,1024]{1,0:T(8,128)}, f32[256,128]{1,0:T(8,128)}, f32[256,512]{1,0:T(8,128)}), (f32[256,256]{0,1:T(8,128)}, f32[256,256]{0,1:T(8,128)}, ...) | async-done | bytes 2228240 | tf_op jit(solution)/shard_map/psum | solution.py:61
  888.2 11.7 cholesky.501
  910.0 20.9 %custom-call.42 = f32[2,128,128]{1,2,0:T(8,128)S(1)} custom-call(f32[2,128,128]{2,1,0:T(8,128)} %copy-done.63), custom_call_target="InvertDiagBlocksLowerTriangular" | custom-call | tf_op jit(solution)/shard_map/triangular_solve/custom-call.5 | solution.py:65
  975.5 11.9 cholesky.535
  997.6 20.5 %custom-call.44 = f32[2,128,128]{1,2,0:T(8,128)S(1)} custom-call(f32[2,128,128]{2,1,0:T(8,128)} %copy-done.64), custom_call_target="InvertDiagBlocksLowerTriangular" | custom-call | tf_op jit(solution)/shard_map/triangular_solve/custom-call.0 | solution.py:58
  1048.1 136.4 %all-reduce.14.cloned.1.call-done = (f32[256,256]{0,1:T(8,128)}, f32[256,256]{0,1:T(8,128)}, f32[256,1024]{1,0:T(8,128)}, f32[256,128]{1,0:T(8,128)}, f32[256,768]{1,0:T(8,128)}) async-done(((f32[256,256]{0,1:T(8,128)}, f32[256,256]{0,1:T(8,128)}, f32[256,1024]{1,0:T(8,128)}, f32[256,128]{1,0:T(8,128)}, f32[256,768]{1,0:T(8,128)}), (f32[256,256]{0,1:T(8,128)}, f32[256,256]{0,1:T(8,128)}, ...) | async-done | bytes 2490384 | tf_op jit(solution)/shard_map/psum | solution.py:61
  1207.7 11.7 cholesky.552
  1229.7 11.7 cholesky.569
  1248.9 20.9 %custom-call.47 = f32[2,128,128]{1,2,0:T(8,128)S(1)} custom-call(f32[2,128,128]{2,1,0:T(8,128)} %copy-done.65), custom_call_target="InvertDiagBlocksLowerTriangular" | custom-call | tf_op jit(solution)/shard_map/triangular_solve/custom-call.5 | solution.py:65
  1311.1 11.9 cholesky.603
  1329.6 19.7 %custom-call.49 = f32[2,128,128]{1,2,0:T(8,128)S(1)} custom-call(f32[2,128,128]{2,1,0:T(8,128)S(1)} %get-tuple-element.95), custom_call_target="InvertDiagBlocksLowerTriangular" | custom-call | tf_op jit(solution)/shard_map/triangular_solve/custom-call.0 | solution.py:58
  1359.2 126.7 %all-reduce.12.cloned.1.call-done = (f32[256,256]{0,1:T(8,128)}, f32[256,256]{0,1:T(8,128)}) async-done(((f32[256,256]{0,1:T(8,128)}, f32[256,256]{0,1:T(8,128)}), (f32[256,256]{0,1:T(8,128)}, f32[256,256]{0,1:T(8,128)})) %all-reduce.12.cloned.1.call-update) | async-done | bytes 524304 | tf_op jit(solution)/shard_map/psum | solution.py:61
  1492.2 11.9 cholesky.620
  1516.1 11.7 cholesky.637
  1536.0 20.7 %custom-call.52 = f32[2,128,128]{1,2,0:T(8,128)S(1)} custom-call(f32[2,128,128]{2,1,0:T(8,128)} %copy-done.59), custom_call_target="InvertDiagBlocksLowerTriangular" | custom-call | tf_op jit(solution)/shard_map/triangular_solve/custom-call.5 | solution.py:65
  (479 shorter events, 571.1 us)
Async XLA Ops:
  7.2 144.9 %all-reduce.20.cloned.1.call-start = ((), (), s32[]{:S(2)}) async-start(), calls=%async_computation.8 | async-start | bytes 2359296 | tf_op jit(solution)/shard_map/psum | solution.py:45
  10.1 165.6 %copy-start.66 = (f32[1,256]{1,0:T(1,128)}, f32[1,256]{1,0:T(1,128)S(1)}, u32[]{:S(2)}) copy-start(f32[1,256]{1,0:T(1,128)S(1)} %get-tuple-element.251) | copy-start | bytes 3076
  10.2 165.6 %copy-start.74 = (pred[256]{0:T(512)(128)(4,1)}, pred[256]{0:T(512)(128)(4,1)S(1)}, u32[]{:S(2)}) copy-start(pred[256]{0:T(512)(128)(4,1)S(1)} %get-tuple-element.279) | copy-start | bytes 772
  10.2 5.1 copy-start
  18.0 225.5 %all-gather.9.cloned.1.call-start = ((), (), s32[]{:S(2)}) async-start(), calls=%async_computation | async-start | bytes 8650752 | tf_op jit(solution)/shard_map/all_gather | solution.py:56
  152.0 10.0 copy-start.57
  166.9 306.1 %all-reduce.18.cloned.1.call-start = ((), (), s32[]{:S(2)}) async-start(), calls=%async_computation.7 | async-start | bytes 3932160 | tf_op jit(solution)/shard_map/psum | solution.py:61
  338.9 248.6 %all-gather.11.cloned.1.call-start = ((), (), s32[]{:S(2)}) async-start(), calls=%async_computation.1 | async-start | bytes 8650752 | tf_op jit(solution)/shard_map/all_gather | solution.py:56
  473.0 10.1 copy-start.55
  491.6 336.1 %all-reduce.16.cloned.1.call-start = ((), (), s32[]{:S(2)}) async-start(), calls=%async_computation.6 | async-start | bytes 4456448 | tf_op jit(solution)/shard_map/psum | solution.py:61
  499.0 6.6 copy-start.33
  666.9 5.0 copy-start.14
  691.7 249.5 %all-gather.13.cloned.1.call-start = ((), (), s32[]{:S(2)}) async-start(), calls=%async_computation.2 | async-start | bytes 8650752 | tf_op jit(solution)/shard_map/all_gather | solution.py:56
  827.7 10.4 copy-start.56
  848.4 336.1 %all-reduce.14.cloned.1.call-start = ((), (), s32[]{:S(2)}) async-start(), calls=%async_computation.5 | async-start | bytes 4980736 | tf_op jit(solution)/shard_map/psum | solution.py:61
  854.6 5.1 copy-start.34
  1040.8 5.1 copy-start.71
  1048.1 236.7 %all-gather.15.cloned.1.call-start = ((), (), s32[]{:S(2)}) async-start(), calls=%async_computation.3 | async-start | bytes 8650752 | tf_op jit(solution)/shard_map/all_gather | solution.py:56
  1184.5 10.4 copy-start.54
  1207.1 36.9 %copy-start.77 = (s32[2,2]{1,0:T(2,128)S(1)}, s32[2,2]{1,0:T(2,128)}, u32[]{:S(2)}) copy-start(s32[2,2]{1,0:T(2,128)} %get-tuple-element.747) | copy-start | bytes 52
  1207.2 278.8 %all-reduce.12.cloned.1.call-start = ((), (), s32[]{:S(2)}) async-start(), calls=%async_computation.4 | async-start | bytes 1048576 | tf_op jit(solution)/shard_map/psum | solution.py:61
  1244.0 29.4 %copy-start.20 = (f32[128,2048]{1,0:T(8,128)S(1)}, f32[128,2048]{1,0:T(8,128)}, u32[]{:S(2)}) copy-start(f32[128,2048]{1,0:T(8,128)} %copy-done.19) | copy-start | bytes 3145732
  1244.0 29.4 %copy-start.23 = (f32[2048,256]{1,0:T(8,128)S(1)}, f32[2048,256]{1,0:T(8,128)}, u32[]{:S(2)}) copy-start(f32[2048,256]{1,0:T(8,128)} %convolution_subtract_fusion.3) | copy-start | bytes 6291460
  1288.9 60.4 %copy-start.13 = (f32[2048,256]{0,1:T(8,128)S(1)}, f32[2048,256]{0,1:T(8,128)}, u32[]{:S(2)}) copy-start(f32[2048,256]{0,1:T(8,128)} %copy-done.12) | copy-start | bytes 6291460
  (63 other events, 150.5 us)
Sparse Core Ops, SparseCore 0:
  18.1 133.8 all-reduce.19
  167.0 76.4 all-gather.8
  339.1 133.9 all-reduce.17
  491.8 76.5 all-gather.10
  691.8 135.8 all-reduce.15
  848.6 76.7 all-gather.12
  1048.2 136.2 all-reduce.13
  1207.3 77.4 all-gather.14
  1359.4 126.5 all-reduce.11
